TPU v7x, 128 devices: a whole 4x4x4 slice. The times are simulated.
128 devices in a mesh: replica: 8 (over y, z_hi), shard: 16 (over z_lo, x, core).
Axes of the slice: x: 4, y: 4, z: 4 (z_hi: 2, z_lo: 2; z = z_hi * 2 + z_lo), core: 2. Of those that a mesh axis runs over, the one named last changes fastest.
Arguments:
- images: float32 [384, 7, 7, 1024], P(('replica', 'shard')), may hold values from -6 to 6
- filters: float32 [1, 1024, 9216], P(None, 'shard'), may hold values from -0.0625 to 0.0625
- out_grad: float32 [384, 7, 7, 1024], P(('replica', 'shard')), may hold values from -6 to 6
Outputs:
- conv_out: float32 [384, 7, 7, 1024], P(('replica', 'shard'))
- filter_grad: float32 [1, 1024, 9216], P(None, 'shard', 'replica')
All inputs are finite; a program needn't handle non-finite values.
Results may differ from a plain program's by a relative error of at most 0.0003.
Values sent between devices are 32-bit elements; how exact they have to be, the bound alone decides.
A program may use at most 256 MiB of HBM per device.

v0:
```python
import jax
import jax.numpy as jnp
from jax import lax
from jax.sharding import PartitionSpec as P


def tap_terms(piece, grad_own, weight):
    count, rows, cols, width = piece.shape
    owned = weight.shape[0]
    padded = jnp.pad(piece, ((0, 0), (1, 1), (1, 1), (0, 0)))
    flat_grad = grad_own.reshape(-1, owned)
    output = jnp.zeros((count * rows * cols, owned), jnp.float32)
    pieces = []
    for a in range(3):
        for c in range(3):
            tap = 3 * a + c
            shifted = padded[:, a : a + rows, c : c + cols, :].reshape(-1, width)
            wslice = weight[:, tap * width : (tap + 1) * width]
            output = output + lax.dot_general(
                shifted,
                wslice,
                (((1,), (1,)), ((), ())),
                precision=lax.Precision.HIGHEST,
                preferred_element_type=jnp.float32,
            )
            pieces.append(
                lax.dot_general(
                    flat_grad,
                    shifted,
                    (((0,), (0,)), ((), ())),
                    precision=lax.Precision.HIGHEST,
                    preferred_element_type=jnp.float32,
                )
            )
    grad = jnp.stack(pieces, axis=0).transpose(1, 0, 2).reshape(owned, 9 * width)
    return (output.reshape(count, rows, cols, owned), grad)


def add_block(piece, grad_own, filters):
    output, grad = tap_terms(piece, grad_own[:, :, :, 0, :], filters[0])
    outs = [output]
    grads = [grad]
    stacked = jnp.stack(outs, axis=3)
    return (stacked, jnp.stack(grads, axis=0))


def on_device(images, filters, out_grad):
    img_dev, rows, cols, chans = images.shape
    groups, owned, kdim = filters.shape
    width = kdim // 9
    shaped = out_grad.reshape(img_dev, rows, cols, groups, width)
    grad_mine = lax.all_to_all(shaped, "shard", split_axis=4, concat_axis=0, tiled=True)
    conv_buf, grad_sum = add_block(
        lax.all_gather(images, "shard", axis=0, tiled=True), grad_mine, filters
    )
    returned = lax.all_to_all(conv_buf, "shard", split_axis=0, concat_axis=4, tiled=True)
    conv_out = returned.reshape(img_dev, rows, cols, chans)
    total = lax.psum(grad_sum, "replica")
    span = kdim // lax.axis_size("replica")
    filter_grad = lax.dynamic_slice_in_dim(total, lax.axis_index("replica") * span, span, 2)
    return (conv_out, filter_grad)


def solution(mesh):
    return jax.shard_map(
        on_device,
        mesh=mesh,
        in_specs=(
            P(("replica", "shard"), None, None, None),
            P(None, "shard", None),
            P(("replica", "shard"), None, None, None),
        ),
        out_specs=(P(("replica", "shard"), None, None, None), P(None, "shard", "replica")),
        check_vma=False,
    )
```

profile of v0, /device:TPU:0, one launch (start us, length us, event | category | flops | bytes accessed | tf_op | source)
XLA Modules:
  0.0 583.9 jit_solution(415974414344355399)
XLA Ops:
  7.2 0.0 all-gather.2.cloned.1.call-start
  7.2 0.7 all-gather.2.cloned.1.call-update
  7.9 0.0 all-reduce.3.cloned.1.call-start
  7.9 23.6 %copy.27 = f32[3,7,7,1,1024]{2,3,1,0,4:T(1,128)} copy(f32[3,7,7,1,1024]{4,2,1,0,3:T(8,128)} %bitcast.125) | data formatting | bytes 1204224 | tf_op jit(solution)/shard_map/reshape | solution.py:51
  31.6 0.5 broadcast.3
  32.1 35.0 %reduce.4 = f32[1024,3,7,7]{3,2,1,0:T(8,128)} reduce(f32[1024,3,7,1,7]{4,3,2,1,0:T(1,128)} %bitcast.112, f32[]{:T(128)} %broadcast.3), dimensions={3}, to_apply=%bitcast.67.reduce_sub_computation | reduce | bytes 1204228
  67.1 9.2 %reshape.53 = f32[16,1,9408]{2,1,0:T(1,128)S(1)} reshape(f32[1024,3,7,7]{3,2,1,0:T(8,128)} %reduce.4) | data formatting | bytes 1204224
  76.3 17.5 %all_to_all.30 = f32[16,1,9408]{2,1,0:T(1,128)S(1)} all-to-all(f32[16,1,9408]{2,1,0:T(1,128)S(1)} %reshape.53), channel_id=1, replica_groups=mesh['replica'=8,'shard'=16] {'shard'}, dimensions={0} | all-to-all | bytes 1204224 | tf_op jit(solution)/shard_map/all_to_all | solution.py:52
  93.8 2.1 reduce.5
  95.9 19.8 %reshape.54 = f32[1024,3,7,1,7]{4,3,2,1,0:T(1,128)} reshape(f32[16,9408]{1,0:T(8,128)S(1)} %reduce.5) | data formatting | bytes 1204224
  115.7 37.1 %bitcast_reduce_fusion = f32[3,7,7,1024]{2,1,0,3:T(8,128)} fusion(f32[1024,3,7,1,7]{4,3,2,1,0:T(1,128)} %reshape.54), kind=kLoop, calls=%fused_computation.45 | loop fusion | bytes 1204224 | tf_op jit(solution)/shard_map/all_to_all | solution.py:52
  152.8 7.6 %copy.32 = f32[3,7,7,1,16,64]{5,4,3,2,1,0:T(8,128)S(1)} copy(f32[3,7,7,1,16,64]{2,1,0,5,4,3:T(8,128)} %bitcast.111) | data formatting | bytes 1204224 | tf_op jit(solution)/shard_map/all_to_all | solution.py:52
  160.4 0.4 copy.29
  160.9 0.1 reshape_squeeze.3
  161.0 0.0 all-gather.2.cloned.1.call-done
  161.0 57.5 %pad_slice_fusion = (f32[48,7,7,1024]{3,2,1,0:T(8,128)}, f32[48,7,7,1024]{3,2,1,0:T(8,128)}, f32[48,7,7,1024]{3,2,1,0:T(8,128)}, f32[48,7,7,1024]{3,2,1,0:T(8,12...) fusion(f32[48,7,7,1024]{3,2,1,0:T(8,128)} %all-gather.2.cloned., ...), kind=kLoop, calls=%fused_computation | loop fusion | bytes 86704128 | tf_op jit(solution)/shard_map/slice | solution.py:17
  218.5 11.0 %reshape.47 = f32[2352,1024]{1,0:T(8,128)} reshape(f32[48,7,7,1024]{3,2,1,0:T(8,128)} %get-tuple-element.2) | data formatting | bytes 19267584 | tf_op jit(solution)/shard_map/reshape | solution.py:17
  229.5 10.9 %reshape.40 = f32[2352,1024]{1,0:T(8,128)} reshape(f32[48,7,7,1024]{3,2,1,0:T(8,128)} %get-tuple-element.3) | data formatting | bytes 19267584 | tf_op jit(solution)/shard_map/reshape | solution.py:17
  240.4 10.9 %reshape.41 = f32[2352,1024]{1,0:T(8,128)} reshape(f32[48,7,7,1024]{3,2,1,0:T(8,128)} %get-tuple-element.4) | data formatting | bytes 19267584 | tf_op jit(solution)/shard_map/reshape | solution.py:17
  251.3 10.9 %reshape.42 = f32[2352,1024]{1,0:T(8,128)} reshape(f32[48,7,7,1024]{3,2,1,0:T(8,128)} %get-tuple-element.5) | data formatting | bytes 19267584 | tf_op jit(solution)/shard_map/reshape | solution.py:17
  262.3 11.0 %reshape.44 = f32[2352,1024]{1,0:T(8,128)} reshape(f32[48,7,7,1024]{3,2,1,0:T(8,128)} %get-tuple-element.6) | data formatting | bytes 19267584 | tf_op jit(solution)/shard_map/reshape | solution.py:17
  273.2 11.0 %reshape.45 = f32[2352,1024]{1,0:T(8,128)} reshape(f32[48,7,7,1024]{3,2,1,0:T(8,128)} %get-tuple-element.7) | data formatting | bytes 19267584 | tf_op jit(solution)/shard_map/reshape | solution.py:17
  284.2 10.9 %reshape.46 = f32[2352,1024]{1,0:T(8,128)} reshape(f32[48,7,7,1024]{3,2,1,0:T(8,128)} %get-tuple-element.8) | data formatting | bytes 19267584 | tf_op jit(solution)/shard_map/reshape | solution.py:17
  295.1 11.0 %reshape.39 = f32[2352,1024]{1,0:T(8,128)} reshape(f32[48,7,7,1024]{3,2,1,0:T(8,128)} %get-tuple-element.9) | data formatting | bytes 19267584 | tf_op jit(solution)/shard_map/reshape | solution.py:17
  306.1 14.4 %fusion.17 = f32[2352,64]{0,1:T(8,128)S(1)} fusion(f32[2352,1024]{1,0:T(8,128)} %reshape.39, f32[64,9216]{1,0:T(8,128)} %bitcast.116), kind=kOutput, calls=%fused_computation.42 | convolution fusion | flops 1849688064 | bytes 10498048 | tf_op jit(solution)/shard_map/dot_general | solution.py:19
  320.5 0.0 slice-start.20
  320.6 7.1 %fusion.8 = f32[9,64,1024]{2,1,0:T(8,128)} fusion(f32[2352,1024]{1,0:T(8,128)S(1)} %copy-done, f32[2352,64]{1,0:T(8,128)S(1)} %reshape_squeeze.3), kind=kOutput, calls=%fused_computation.33 | convolution fusion | flops 1849688064 | bytes 10498048 | tf_op jit(solution)/shard_map/dot_general | solution.py:27
  327.7 0.0 slice-start.16
  327.7 7.1 %fusion.7 = f32[9,64,1024]{2,1,0:T(8,128)} fusion(f32[9,64,1024]{2,1,0:T(8,128)} %fusion.8, f32[2352,1024]{1,0:T(8,128)S(1)} %bitcast.110, f32[2352,64]{1,0:T(8,128)S(1)} %reshape_squeeze.3), kind=kOutput, calls=%fused_computation.31 | convolution fusion | flops 1849688064 | bytes 10498048 | tf_op jit(solution)/shard_map/dot_general | solution.py:27
  334.8 10.6 %convolution_add_fusion.7 = f32[2352,64]{0,1:T(8,128)S(1)} fusion(f32[2352,64]{0,1:T(8,128)S(1)} %fusion.17, f32[2352,1024]{1,0:T(8,128)S(1)} %bitcast.110, f32[64,9216]{1,0:T(8,128)} %bitcast.117), kind=kOutput, calls=%fused_computation.15 | convolution fusion | flops 1849838592 | bytes 11100160 | tf_op jit(solution)/shard_map/dot_general | solution.py:19
  345.5 0.0 slice-start.12
  345.5 10.7 %convolution_add_fusion.6 = f32[2352,64]{0,1:T(8,128)S(1)} fusion(f32[2352,64]{0,1:T(8,128)S(1)} %convolution_add_fusion.7, f32[2352,1024]{1,0:T(8,128)S(1)} %bitcast.108, f32[64,9216]{1,0:T(8,128)} %bitcast.118), kind=kOutput, calls=%fused_computation.14 | convolution fusion | flops 1849838592 | bytes 11100160 | tf_op jit(solution)/shard_map/dot_general | solution.py:19
  356.2 0.0 slice-start.14
  356.2 7.1 %fusion.6 = f32[9,64,1024]{2,1,0:T(8,128)} fusion(f32[9,64,1024]{2,1,0:T(8,128)} %fusion.7, f32[2352,1024]{1,0:T(8,128)S(1)} %bitcast.108, f32[2352,64]{1,0:T(8,128)S(1)} %reshape_squeeze.3), kind=kOutput, calls=%fused_computation.29 | convolution fusion | flops 1849688064 | bytes 10498048 | tf_op jit(solution)/shard_map/dot_general | solution.py:27
  363.4 7.5 %fusion.5 = f32[9,64,1024]{2,1,0:T(8,128)} fusion(f32[9,64,1024]{2,1,0:T(8,128)} %fusion.6, f32[2352,1024]{1,0:T(8,128)S(1)} %bitcast.106, f32[2352,64]{1,0:T(8,128)S(1)} %reshape_squeeze.3), kind=kOutput, calls=%fused_computation.27 | convolution fusion | flops 1849688064 | bytes 10498048 | tf_op jit(solution)/shard_map/dot_general | solution.py:27
  370.9 10.3 %convolution_add_fusion.5 = f32[2352,64]{0,1:T(8,128)S(1)} fusion(f32[2352,64]{0,1:T(8,128)S(1)} %convolution_add_fusion.6, f32[2352,1024]{1,0:T(8,128)S(1)} %bitcast.106, f32[64,9216]{1,0:T(8,128)} %bitcast.119), kind=kOutput, calls=%fused_computation.13 | convolution fusion | flops 1849838592 | bytes 11100160 | tf_op jit(solution)/shard_map/dot_general | solution.py:19
  381.3 11.0 %reshape.43 = f32[2352,1024]{1,0:T(8,128)} reshape(f32[48,7,7,1024]{3,2,1,0:T(8,128)} %all-gather.2.cloned.1.call-done) | data formatting | bytes 19267584 | tf_op jit(solution)/shard_map/reshape | solution.py:17
  392.3 14.2 %convolution_add_fusion.4 = f32[2352,64]{0,1:T(8,128)S(1)} fusion(f32[2352,64]{0,1:T(8,128)S(1)} %convolution_add_fusion.5, f32[2352,1024]{1,0:T(8,128)} %reshape.43, f32[64,9216]{1,0:T(8,128)} %bitcast.120), kind=kOutput, calls=%fused_computation.12 | convolution fusion | flops 1849838592 | bytes 11100160 | tf_op jit(solution)/shard_map/dot_general | solution.py:19
  406.5 6.8 %fusion.4 = f32[9,64,1024]{2,1,0:T(8,128)} fusion(f32[9,64,1024]{2,1,0:T(8,128)} %fusion.5, f32[2352,64]{1,0:T(8,128)S(1)} %reshape_squeeze.3, f32[2352,1024]{1,0:T(8,128)S(1)} %copy-done.1), kind=kOutput, calls=%fused_computation.25 | convolution fusion | flops 1849688064 | bytes 10498048 | tf_op jit(solution)/shard_map/dot_general | solution.py:27
  413.3 10.0 %fusion.3 = f32[9,64,1024]{2,1,0:T(8,128)} fusion(f32[9,64,1024]{2,1,0:T(8,128)} %fusion.4, f32[2352,1024]{1,0:T(8,128)} %reshape.44, f32[2352,64]{1,0:T(8,128)S(1)} %reshape_squeeze.3), kind=kOutput, calls=%fused_computation.23 | convolution fusion | flops 1849688064 | bytes 10498048 | tf_op jit(solution)/shard_map/dot_general | solution.py:27
  423.4 0.0 slice-start.8
  423.4 0.0 slice-start
  423.4 7.2 %fusion.2 = f32[9,64,1024]{2,1,0:T(8,128)} fusion(f32[9,64,1024]{2,1,0:T(8,128)} %fusion.3, f32[2352,1024]{1,0:T(8,128)S(1)} %bitcast.104, f32[2352,64]{1,0:T(8,128)S(1)} %reshape_squeeze.3), kind=kOutput, calls=%fused_computation.21 | convolution fusion | flops 1849688064 | bytes 10498048 | tf_op jit(solution)/shard_map/dot_general | solution.py:27
  430.6 7.1 %fusion.1 = f32[9,64,1024]{2,1,0:T(8,128)} fusion(f32[9,64,1024]{2,1,0:T(8,128)} %fusion.2, f32[2352,1024]{1,0:T(8,128)S(1)} %bitcast.102, f32[2352,64]{1,0:T(8,128)S(1)} %reshape_squeeze.3), kind=kOutput, calls=%fused_computation.19 | convolution fusion | flops 1849688064 | bytes 10498048 | tf_op jit(solution)/shard_map/dot_general | solution.py:27
  437.7 7.5 %fusion = f32[9,64,1024]{2,1,0:T(8,128)} fusion(f32[9,64,1024]{2,1,0:T(8,128)} %fusion.1, f32[2352,1024]{1,0:T(8,128)S(1)} %bitcast.98, f32[2352,64]{1,0:T(8,128)S(1)} %reshape_squeeze.3), kind=kOutput, calls=%fused_computation.17 | convolution fusion | flops 1849688064 | bytes 10498048 | tf_op jit(solution)/shard_map/dot_general | solution.py:27
  445.3 5.1 copy.30
  450.4 4.5 stack_reshape.7
  454.8 0.0 all-reduce.3.cloned.1.call-update
  454.9 13.0 %convolution_add_fusion.3 = f32[2352,64]{0,1:T(8,128)S(1)} fusion(f32[2352,64]{0,1:T(8,128)S(1)} %convolution_add_fusion.4, f32[2352,1024]{1,0:T(8,128)} %reshape.44, f32[64,9216]{1,0:T(8,128)} %bitcast.121), kind=kOutput, calls=%fused_computation.11 | convolution fusion | flops 1849838592 | bytes 11100160 | tf_op jit(solution)/shard_map/dot_general | solution.py:19
  467.9 0.0 slice-start.4
  467.9 13.3 %convolution_add_fusion.2 = f32[2352,64]{0,1:T(8,128)S(1)} fusion(f32[2352,64]{0,1:T(8,128)S(1)} %convolution_add_fusion.3, f32[2352,1024]{1,0:T(8,128)} %reshape.45, f32[64,9216]{1,0:T(8,128)} %bitcast.122), kind=kOutput, calls=%fused_computation.10 | convolution fusion | flops 1849838592 | bytes 11100160 | tf_op jit(solution)/shard_map/dot_general | solution.py:19
  481.2 13.3 %convolution_add_fusion.1 = f32[2352,64]{0,1:T(8,128)S(1)} fusion(f32[2352,64]{0,1:T(8,128)S(1)} %convolution_add_fusion.2, f32[2352,1024]{1,0:T(8,128)} %reshape.46, f32[64,9216]{1,0:T(8,128)} %bitcast.123), kind=kOutput, calls=%fused_computation.9 | convolution fusion | flops 1849838592 | bytes 11100160 | tf_op jit(solution)/shard_map/dot_general | solution.py:19
  494.5 10.3 %convolution_add_fusion = f32[2352,64]{0,1:T(8,128)S(1)} fusion(f32[2352,64]{0,1:T(8,128)S(1)} %convolution_add_fusion.1, f32[2352,1024]{1,0:T(8,128)S(1)} %bitcast.100, f32[64,9216]{1,0:T(8,128)} %bitcast.124), kind=kOutput, calls=%fused_computation.8 | convolution fusion | flops 1849838592 | bytes 11100160 | tf_op jit(solution)/shard_map/dot_general | solution.py:19
  504.9 0.4 copy.24
  505.2 3.7 reduce.2
  508.9 1.8 reshape.51
  510.7 3.8 all-to-all-start
  514.5 11.7 %all-to-all-done = f32[16,1,9408]{2,1,0:T(1,128)S(1)} async-done(((f32[16,1,9408]{2,1,0:T(1,128)}), f32[16,1,9408]{2,1,0:T(1,128)S(1)}, u32[]{:S(2)}, u32[]{:S(2)}) %all-to-all-start) | async-done | bytes 602144 | tf_op jit(solution)/shard_map/all_to_all | solution.py:56
  526.2 2.1 reduce.3
  528.3 1.2 reshape.52
  529.6 0.1 copy.26
  529.7 1.2 reshape.48
  530.9 44.2 %all-reduce.3.cloned.1.call-done = f32[1,64,9216]{2,1,0:T(8,128)} async-done(((f32[1,64,9216]{2,1,0:T(8,128)}), f32[1,64,9216]{2,1,0:T(8,128)}) %all-reduce.3.cloned.1.call-update) | async-done | bytes 2359312 | tf_op jit(solution)/shard_map/psum | solution.py:58
  575.1 1.7 constant_dynamic-slice_fusion
  (46 shorter events, 0.1 us)
Async XLA Ops:
  7.2 153.9 %all-gather.2.cloned.1.call-start = ((), (), s32[]{:S(2)}) async-start(), calls=%async_computation.2 | async-start | bytes 11698176 | tf_op jit(solution)/shard_map/all_gather | solution.py:54
  7.9 567.2 %all-reduce.3.cloned.1.call-start = ((), (), s32[]{:S(2)}) async-start(), calls=%async_computation.3 | async-start | bytes 4718592 | tf_op jit(solution)/shard_map/psum | solution.py:58
  306.1 14.5 %copy-start = (f32[2352,1024]{1,0:T(8,128)S(1)}, f32[2352,1024]{1,0:T(8,128)}, u32[]{:S(2)}) copy-start(f32[2352,1024]{1,0:T(8,128)} %reshape.39) | copy-start | bytes 28901380
  306.1 21.6 %slice-start.18 = ((s8[9633792]{0:T(1024)(128)(4,1)}), s8[4194304]{0:T(1024)(128)(4,1)S(1)}, s32[]{:S(2)}) async-start(s8[9633792]{0:T(1024)(128)(4,1)} %bitcast.109), calls=%async_computation.22 | async-start | bytes 8388608
  306.1 21.6 %slice-start.19 = ((s8[9633792]{0:T(1024)(128)(4,1)}), s8[4194304]{0:T(1024)(128)(4,1)S(1)}, s32[]{:S(2)}) async-start(s8[9633792]{0:T(1024)(128)(4,1)} %bitcast.109), calls=%async_computation.23 | async-start | bytes 8388608
  320.5 7.1 %slice-start.20 = ((s8[9633792]{0:T(1024)(128)(4,1)}), s8[1245184]{0:T(1024)(128)(4,1)S(1)}, s32[]{:S(2)}) async-start(s8[9633792]{0:T(1024)(128)(4,1)} %bitcast.109), calls=%async_computation.24 | async-start | bytes 2490368
  327.7 17.8 %slice-start.15 = ((s8[9633792]{0:T(1024)(128)(4,1)}), s8[4194304]{0:T(1024)(128)(4,1)S(1)}, s32[]{:S(2)}) async-start(s8[9633792]{0:T(1024)(128)(4,1)} %bitcast.107), calls=%async_computation.19 | async-start | bytes 8388608
  327.7 17.8 %slice-start.16 = ((s8[9633792]{0:T(1024)(128)(4,1)}), s8[4194304]{0:T(1024)(128)(4,1)S(1)}, s32[]{:S(2)}) async-start(s8[9633792]{0:T(1024)(128)(4,1)} %bitcast.107), calls=%async_computation.20 | async-start | bytes 8388608
  334.8 10.6 %slice-start.17 = ((s8[9633792]{0:T(1024)(128)(4,1)}), s8[1245184]{0:T(1024)(128)(4,1)S(1)}, s32[]{:S(2)}) async-start(s8[9633792]{0:T(1024)(128)(4,1)} %bitcast.107), calls=%async_computation.21 | async-start | bytes 2490368
  345.5 17.9 %slice-start.12 = ((s8[9633792]{0:T(1024)(128)(4,1)}), s8[4194304]{0:T(1024)(128)(4,1)S(1)}, s32[]{:S(2)}) async-start(s8[9633792]{0:T(1024)(128)(4,1)} %bitcast.105), calls=%async_computation.16 | async-start | bytes 8388608
  345.5 17.9 %slice-start.13 = ((s8[9633792]{0:T(1024)(128)(4,1)}), s8[4194304]{0:T(1024)(128)(4,1)S(1)}, s32[]{:S(2)}) async-start(s8[9633792]{0:T(1024)(128)(4,1)} %bitcast.105), calls=%async_computation.17 | async-start | bytes 8388608
  356.2 7.2 %slice-start.14 = ((s8[9633792]{0:T(1024)(128)(4,1)}), s8[1245184]{0:T(1024)(128)(4,1)S(1)}, s32[]{:S(2)}) async-start(s8[9633792]{0:T(1024)(128)(4,1)} %bitcast.105), calls=%async_computation.18 | async-start | bytes 2490368
  392.3 14.2 %copy-start.1 = (f32[2352,1024]{1,0:T(8,128)S(1)}, f32[2352,1024]{1,0:T(8,128)}, u32[]{:S(2)}) copy-start(f32[2352,1024]{1,0:T(8,128)} %reshape.43) | copy-start | bytes 28901380
  406.5 16.9 %slice-start.9 = ((s8[9633792]{0:T(1024)(128)(4,1)}), s8[4194304]{0:T(1024)(128)(4,1)S(1)}, s32[]{:S(2)}) async-start(s8[9633792]{0:T(1024)(128)(4,1)} %bitcast.103), calls=%async_computation.13 | async-start | bytes 8388608
  406.5 16.9 %slice-start.10 = ((s8[9633792]{0:T(1024)(128)(4,1)}), s8[4194304]{0:T(1024)(128)(4,1)S(1)}, s32[]{:S(2)}) async-start(s8[9633792]{0:T(1024)(128)(4,1)} %bitcast.103), calls=%async_computation.14 | async-start | bytes 8388608
  413.3 10.0 %slice-start.11 = ((s8[9633792]{0:T(1024)(128)(4,1)}), s8[1245184]{0:T(1024)(128)(4,1)S(1)}, s32[]{:S(2)}) async-start(s8[9633792]{0:T(1024)(128)(4,1)} %bitcast.103), calls=%async_computation.15 | async-start | bytes 2490368
  413.3 17.2 %slice-start.6 = ((s8[9633792]{0:T(1024)(128)(4,1)}), s8[4194304]{0:T(1024)(128)(4,1)S(1)}, s32[]{:S(2)}) async-start(s8[9633792]{0:T(1024)(128)(4,1)} %bitcast.101), calls=%async_computation.10 | async-start | bytes 8388608
  413.3 17.2 %slice-start.7 = ((s8[9633792]{0:T(1024)(128)(4,1)}), s8[4194304]{0:T(1024)(128)(4,1)S(1)}, s32[]{:S(2)}) async-start(s8[9633792]{0:T(1024)(128)(4,1)} %bitcast.101), calls=%async_computation.11 | async-start | bytes 8388608
  423.4 7.2 %slice-start.8 = ((s8[9633792]{0:T(1024)(128)(4,1)}), s8[1245184]{0:T(1024)(128)(4,1)S(1)}, s32[]{:S(2)}) async-start(s8[9633792]{0:T(1024)(128)(4,1)} %bitcast.101), calls=%async_computation.12 | async-start | bytes 2490368
  423.4 14.3 %slice-start = ((s8[9633792]{0:T(1024)(128)(4,1)}), s8[4194304]{0:T(1024)(128)(4,1)S(1)}, s32[]{:S(2)}) async-start(s8[9633792]{0:T(1024)(128)(4,1)} %bitcast.97), calls=%async_computation.4 | async-start | bytes 8388608
  423.4 14.3 %slice-start.1 = ((s8[9633792]{0:T(1024)(128)(4,1)}), s8[4194304]{0:T(1024)(128)(4,1)S(1)}, s32[]{:S(2)}) async-start(s8[9633792]{0:T(1024)(128)(4,1)} %bitcast.97), calls=%async_computation.5 | async-start | bytes 8388608
  430.6 7.2 %slice-start.2 = ((s8[9633792]{0:T(1024)(128)(4,1)}), s8[1245184]{0:T(1024)(128)(4,1)S(1)}, s32[]{:S(2)}) async-start(s8[9633792]{0:T(1024)(128)(4,1)} %bitcast.97), calls=%async_computation.6 | async-start | bytes 2490368
  467.9 26.6 %slice-start.3 = ((s8[9633792]{0:T(1024)(128)(4,1)}), s8[4194304]{0:T(1024)(128)(4,1)S(1)}, s32[]{:S(2)}) async-start(s8[9633792]{0:T(1024)(128)(4,1)} %bitcast.99), calls=%async_computation.7 | async-start | bytes 8388608
  467.9 26.6 %slice-start.4 = ((s8[9633792]{0:T(1024)(128)(4,1)}), s8[4194304]{0:T(1024)(128)(4,1)S(1)}, s32[]{:S(2)}) async-start(s8[9633792]{0:T(1024)(128)(4,1)} %bitcast.99), calls=%async_computation.8 | async-start | bytes 8388608
  481.2 13.3 %slice-start.5 = ((s8[9633792]{0:T(1024)(128)(4,1)}), s8[1245184]{0:T(1024)(128)(4,1)S(1)}, s32[]{:S(2)}) async-start(s8[9633792]{0:T(1024)(128)(4,1)} %bitcast.99), calls=%async_computation.9 | async-start | bytes 2490368
  510.7 15.5 %all-to-all-start = ((f32[16,1,9408]{2,1,0:T(1,128)}), f32[16,1,9408]{2,1,0:T(1,128)S(1)}, u32[]{:S(2)}, u32[]{:S(2)}) async-start(f32[16,1,9408]{2,1,0:T(1,128)} %reshape.51), calls=%async_computation | async-start | bytes 1212416 | tf_op jit(solution)/shard_map/all_to_all | solution.py:56
Sparse Core Ops, SparseCore 0:
  9.7 66.9 all-gather.1
  455.0 120.0 all-reduce.2
where the time goes:
time: 595 us; the launch traced here: 584 us
  local copies, waits for them, and re-layouts  271 us (46%)
  matrix products  178 us (30%)
  waiting for transfers between devices  56.6 us (10%)
  other arithmetic  42.9 us (7%)
  blocking collectives  17.5 us (3%)
  between operations  14.7 us (2%)
    dot_general x9, matrix products, tap_terms(): lax.dot_general(shifted, wslice, (((1,), (1,)), ((), ())), precision=lax....  110 us
    reshape x9, local copies, waits for them, and re-layouts, tap_terms(): shifted = padded[:, a:a + rows, c:c + cols, :].reshape(-1, width)  98.5 us
    dot_general x9, matrix products, tap_terms(): lax.dot_general(flat_grad, shifted, (((0,), (0,)), ((), ())), precision=l...  67.6 us
    slice x1, local copies, waits for them, and re-layouts, tap_terms(): shifted = padded[:, a:a + rows, c:c + cols, :].reshape(-1, width)  57.5 us
    all_to_all x3, local copies, waits for them, and re-layouts, on_device(): lax.all_to_all(shaped, 'shard', split_axis=4, concat_axis=0, tiled=True)  45.2 us
    psum x1, waiting for transfers between devices, on_device(): total = lax.psum(grad_sum, 'replica')  44.2 us
    unnamed x8, other arithmetic  35 us
    unnamed x50, local copies, waits for them, and re-layouts  32.1 us
  transfers between devices with their start and end apart: 3, of which 2 were waited for; matrix products, arithmetic and copies ran while one was open for 34% of the time, Pallas kernels for 0%

commit v1 on v0

v1 whole, which is shorter than its diff:
```python
import functools

import jax
import jax.numpy as jnp
from jax import lax
from jax.experimental import pallas as pl
from jax.experimental.pallas import tpu as pltpu
from jax.sharding import PartitionSpec as P

MESH = pl.DeviceIdType.MESH
F32 = jnp.float32
BF16 = jnp.bfloat16
NX = 4
NY = 4
NCH = 4
CW = 256
ROWS = 147
WIRE = 152
SLOT = 160
CUT = 80
NSLOT = 16
TOTAL = SLOT * NSLOT
GROUP = 4 * SLOT
OWN = 64
DELTA = [7 * (t // 3 - 1) + (t % 3 - 1) for t in range(9)]

S_OWN, S_A, S_B, S_C, S_D, S_E, S_F, S_G = 0, 2, 4, 6, 8, 10, 12, 14
K_A, K_B, K_C, K_D1, K_D2, K_E, K_F, K_G1, K_G2, K_P = range(10)
NK = K_P + 8
INVERSE = [0, 2, 1, 3, 4, 6, 5, 7]


def kernel(
    x_ref, f_ref, g_ref, out_ref, fg_ref,
    xg, x3, f3t, f8t, gall, gsh, gsl, maskc, maskg, yacc, fgu, r1, r2, sy, fin, zs, zr, cs, cp, cf,
    xsend, xrecv, gsend, grecv, csend, crecv, rsend, rrecv, zsem,
):
    rep = lax.axis_index("replica")
    shard = lax.axis_index("shard")
    core = lax.rem(shard, 2)
    x = lax.rem(lax.div(shard, 2), NX)
    z = lax.div(shard, 2 * NX)
    y = lax.div(rep, 2)
    zh = lax.rem(rep, 2)

    def at(dx, dz, dc=0):
        xx = lax.rem(x + dx + NX, NX)
        zz = lax.rem(z + dz, 2)
        cc = lax.rem(core + dc, 2)
        return (rep, zz * 2 * NX + xx * 2 + cc)

    def chip_of(dx, dz):
        return lax.rem(z + dz, 2) * NX + lax.rem(x + dx + NX, NX)

    rel = [(0, 0), (-1, 0), (1, 0), (0, 1), (2, 0), (-1, 1), (1, 1), (2, 1)]
    partner = at(0, 0, 1)
    yp = lax.rem(y + 1, NY)
    ym = lax.rem(y + NY - 1, NY)
    y2 = lax.rem(y + 2, NY)
    up = (yp * 2 + zh, shard)
    down = (ym * 2 + zh, shard)
    far = (y * 2 + 1 - zh, shard)

    peers = [at(*rel[k]) for k in range(1, 8)] + [partner, up, down, far]
    barrier = pltpu.get_barrier_semaphore()
    for peer in peers:
        pl.semaphore_signal(barrier, inc=1, device_id=peer, device_id_type=MESH)
    pl.semaphore_wait(barrier, len(peers))

    def remote(src, dst, ssem, rsem, dev):
        return pltpu.make_async_remote_copy(
            src_ref=src, dst_ref=dst, send_sem=ssem, recv_sem=rsem, device_id=dev, device_id_type=MESH
        )

    def grad_copy(k):
        if k == 0:
            return None
        cols = pl.ds(pl.multiple_of(128 * chip_of(*rel[k]), 128), 128)
        return remote(g_ref.at[:, cols], gall.at[2 * INVERSE[k]], gsend.at[k], grecv.at[INVERSE[k]], at(*rel[k]))

    def grad_in(k):
        return remote(gall.at[2 * k], gall.at[2 * k], gsend.at[k], grecv.at[k], at(*rel[k]))

    def grad_pass(k):
        if k == 0:
            cols = pl.ds(pl.multiple_of(128 * chip_of(0, 0), 128), 128)
            src = g_ref.at[:, cols]
        else:
            src = gall.at[2 * k]
        return remote(src, gall.at[2 * k + 1], gsend.at[8 + k], grecv.at[8 + k], partner)

    def own(j):
        return x_ref.at[:, pl.ds(pl.multiple_of(CW * j, CW), CW)]

    def x_copy(j, kind):
        lo, hi = pl.ds(0, CUT), pl.ds(CUT, WIRE - CUT)
        if kind >= K_P:
            k = kind - K_P
            src = own(j) if k == 0 else xg.at[j, 2 * k]
            dst, dev = xg.at[j, 2 * k + 1], partner
        elif kind == K_A:
            src, dst, dev = own(j), xg.at[j, S_A], at(1, 0)
        elif kind == K_B:
            src, dst, dev = own(j), xg.at[j, S_B], at(-1, 0)
        elif kind == K_C:
            src, dst, dev = own(j), xg.at[j, S_C], at(0, 1)
        elif kind == K_D1:
            src, dst, dev = xg.at[j, S_A, lo], xg.at[j, S_D, lo], at(1, 0)
        elif kind == K_D2:
            src, dst, dev = xg.at[j, S_B, hi], xg.at[j, S_D, hi], at(-1, 0)
        elif kind == K_E:
            src, dst, dev = xg.at[j, S_C], xg.at[j, S_E], at(1, 0)
        elif kind == K_F:
            src, dst, dev = xg.at[j, S_C], xg.at[j, S_F], at(-1, 0)
        elif kind == K_G1:
            src, dst, dev = xg.at[j, S_D, lo], xg.at[j, S_G, lo], at(0, 1)
        else:
            src, dst, dev = xg.at[j, S_D, hi], xg.at[j, S_G, hi], at(0, 1)
        return remote(src, dst, xsend.at[j, kind], xrecv.at[j, kind], dev)

    def x_own(j):
        for kind in (K_A, K_B, K_C, K_P):
            x_copy(j, kind).start()

    for k in (4, 7, 1, 2, 5, 6, 3):
        grad_copy(k).start()
    grad_pass(0).start()
    x_own(0)
    x_own(1)

    for j in range(NCH):
        xg[j, 0] = x_ref[:, CW * j : CW * (j + 1)]
    gall[0] = g_ref[:, pl.ds(pl.multiple_of(128 * chip_of(0, 0), 128), 128)]

    lane = lax.broadcasted_iota(jnp.int32, (SLOT, 128), 1)
    low = lane < OWN
    pos = lax.broadcasted_iota(jnp.int32, (SLOT, 128), 0).astype(F32)
    rem = pos - 49.0 * jnp.floor((pos + 0.5) * (1.0 / 49.0))
    hh = jnp.floor((rem + 0.5) * (1.0 / 7.0))
    ww = rem - 7.0 * hh
    for pair in range(5):
        t0, t1 = 2 * pair, min(2 * pair + 1, 8)
        da = jnp.where(low, float(t0 // 3 - 1), float(t1 // 3 - 1))
        dc = jnp.where(low, float(t0 % 3 - 1), float(t1 % 3 - 1))
        for sign, mask in ((1.0, maskc), (-1.0, maskg)):
            h1, w1 = hh + sign * da, ww + sign * dc
            inside = jnp.minimum(jnp.minimum(h1, 6.0 - h1), jnp.minimum(w1, 6.0 - w1)) > -0.5
            mask[pair] = jnp.where(inside, 1.0, 0.0)

    def halves(v):
        hi = v.astype(BF16)
        lo = (v - hi.astype(F32)).astype(BF16)
        return hi, lo

    @pl.loop(0, NCH)
    def _(j):
        for pair in range(4):
            parts = []
            for t in (2 * pair, 2 * pair + 1):
                parts.append(f_ref[:, pl.ds(pl.multiple_of(t * 1024 + CW * j, CW), CW)])
            hi, lo = halves(jnp.concatenate(parts, axis=0).T)
            cols = slice(128 * pair, 128 * pair + 128)
            f3t[j, 0:CW, cols] = hi
            f3t[j, CW : 2 * CW, cols] = hi
            f3t[j, 2 * CW : 3 * CW, cols] = lo
        f8 = f_ref[:, pl.ds(pl.multiple_of(8 * 1024 + CW * j, CW), CW)]
        hi8 = f8.astype(BF16).astype(F32)
        both = jnp.concatenate([hi8, f8 - hi8], axis=0).T.astype(BF16)
        f8t[j, 0:CW, :] = both
        f8t[j, CW : 2 * CW, :] = both

    for k in (1, 2, 3, 4, 5, 6, 7):
        grad_in(k).wait_recv()
        grad_pass(k).start()
    for k in range(8):
        grad_pass(k).wait_recv()

    lane4 = lax.broadcasted_iota(jnp.int32, (GROUP, 128), 1)
    low4 = lane4 < OWN
    mine4 = (lane4 < OWN) == (core == 0)

    def padded(v):
        return jnp.concatenate([v, jnp.zeros((SLOT - WIRE, v.shape[1]), v.dtype)], axis=0)

    @pl.loop(0, 4)
    def _(m):
        g = jnp.concatenate([padded(gall[4 * m + i]) for i in range(4)], axis=0)
        gg = jnp.where(mine4, g, pltpu.roll(g, OWN, 1))
        cols = pl.ds(pl.multiple_of(GROUP * m, GROUP), GROUP)
        for pair in range(5):
            t0, t1 = 2 * pair, min(2 * pair + 1, 8)
            first = pltpu.roll(gg, DELTA[t0] % GROUP, 0)
            second = first if t1 == t0 else pltpu.roll(gg, DELTA[t1] % GROUP, 0)
            mask = jnp.concatenate([maskg[pair]] * 4, axis=0)
            hi, lo = halves((jnp.where(low4, first, second) * mask).T)
            gsh[128 * pair : 128 * pair + 128, cols] = hi
            gsl[128 * pair : 128 * pair + 128, cols] = lo

    def window(yy, j):
        return pl.ds(lax.div(9 * yy - j + 3, 4), 3)

    def r_copy(j, kind):
        if kind == 0:
            src, dst, dev = fgu.at[j, 0, window(y2, j)], r1.at[j, 0], up
        elif kind == 1:
            src, dst, dev = fgu.at[j, 1, window(y2, j)], r1.at[j, 1], down
        elif kind == 2:
            src, dst, dev = fgu.at[j, 1, window(yp, j)], r2.at[j, 1], up
        elif kind == 3:
            src, dst, dev = fgu.at[j, 0, window(ym, j)], r2.at[j, 2], down
        elif kind == 4:
            src, dst, dev = sy.at[j, 0], r2.at[j, 0], up
        else:
            src, dst, dev = sy.at[j, 1], r2.at[j, 3], down
        return remote(src, dst, rsend.at[j, kind], rrecv.at[j, kind], dev)

    def rs_mid(j):
        r_copy(j, 0).wait_recv()
        sy[j, 0] = fgu[j, 0, window(yp, j)] + r1[j, 0]
        r_copy(j, 4).start()
        r_copy(j, 1).wait_recv()
        sy[j, 1] = fgu[j, 1, window(ym, j)] + r1[j, 1]
        r_copy(j, 5).start()

    def rs_end(j):
        for kind in (2, 3, 4, 5):
            r_copy(j, kind).wait_recv()
        fin[j, 0] = fgu[j, 0, window(y, j)] + r2[j, 0] + r2[j, 2]
        fin[j, 1] = fgu[j, 1, window(y, j)] + r2[j, 1] + r2[j, 3]

    def nn(a, b):
        return lax.dot_general(a, b, (((1,), (0,)), ((), ())), preferred_element_type=F32)

    def conv(j, first, count):
        @pl.loop(first, first + count)
        def _(m):
            rows = pl.ds(pl.multiple_of(GROUP * m, GROUP), GROUP)
            main = nn(x3[j, rows, :], f3t[j])
            last = nn(x3[j, rows, 0 : 2 * CW], f8t[j])

            @pl.when(j == 0)
            def _():
                yacc[rows, 0:512] = main
                yacc[rows, 512:640] = last

            @pl.when(j > 0)
            def _():
                yacc[rows, 0:512] += main
                yacc[rows, 512:640] += last

    def to_partner(j, *slots):
        for s in slots:
            x_copy(j, K_P + s // 2).start()

    def chunk(j, carry):
        for kind in (K_A, K_B, K_C):
            x_copy(j, kind).wait_recv()
        for kind in (K_D1, K_D2, K_E, K_F):
            x_copy(j, kind).start()
        to_partner(j, S_A, S_B, S_C)

        @pl.when(j < NCH - 2)
        def _():
            x_own(j + 2)

        @pl.when(j > 0)
        def _():
            conv(j - 1, 0, 2)

        x_copy(j, K_D1).wait_recv()
        x_copy(j, K_G1).start()
        x_copy(j, K_D2).wait_recv()
        x_copy(j, K_G2).start()
        x_copy(j, K_E).wait_recv()
        x_copy(j, K_F).wait_recv()
        to_partner(j, S_D, S_E, S_F)

        @pl.when(j > 0)
        def _():
            rs_mid(j - 1)
            conv(j - 1, 2, 2)
            rs_end(j - 1)

        x_copy(j, K_G1).wait_recv()
        x_copy(j, K_G2).wait_recv()
        to_partner(j, S_G)
        for k in range(8):
            x_copy(j, K_P + k).wait_recv()

        @pl.loop(0, NSLOT)
        def _(s):
            hi, lo = halves(padded(xg[j, s]))
            rows = pl.ds(pl.multiple_of(SLOT * s, SLOT), SLOT)
            x3[j, rows, 0:CW] = hi
            x3[j, rows, CW : 2 * CW] = lo
            x3[j, rows, 2 * CW : 3 * CW] = hi

        res = nn(gsh[0:576, :], x3[j, :, 0:CW])
        res += nn(gsl[0:576, :], x3[j, :, 0:CW])
        res += nn(gsh[0:576, :], x3[j, :, CW : 2 * CW])
        for h in range(2):
            for t in range(9):
                fgu[j, h, t] = res[OWN * t : OWN * (t + 1), 128 * h : 128 * (h + 1)]
            fgu[j, h, 9] = jnp.zeros((OWN, 128), F32)
        for kind in (0, 1, 2, 3):
            r_copy(j, kind).start()
        return carry

    lax.fori_loop(0, NCH, chunk, 0)

    conv(NCH - 1, 0, 2)
    rs_mid(NCH - 1)
    conv(NCH - 1, 2, 2)

    @pl.loop(0, 4)
    def _(m):
        rows = pl.ds(pl.multiple_of(GROUP * m, GROUP), GROUP)
        total = jnp.zeros((GROUP, 128), F32)
        for pair in range(5):
            v = yacc[rows, 128 * pair : 128 * pair + 128]
            t0, t1 = 2 * pair, min(2 * pair + 1, 8)
            first = pltpu.roll(v, -DELTA[t0] % GROUP, 0)
            second = first if t1 == t0 else pltpu.roll(v, -DELTA[t1] % GROUP, 0)
            total += jnp.where(low4, first, second) * jnp.concatenate([maskc[pair]] * 4, axis=0)
        total += pltpu.roll(total, OWN, 1)
        for i in range(4):
            cs[4 * m + i] = total[SLOT * i : SLOT * i + WIRE]

    def c_pass(k):
        return remote(cs.at[2 * k + 1], cp.at[k], csend.at[8 + k], crecv.at[8 + k], partner)

    mycols = pl.ds(pl.multiple_of(128 * chip_of(0, 0), 128), 128)

    def c_copy(k):
        return remote(cf.at[k], out_ref.at[:, mycols], csend.at[k], crecv.at[INVERSE[k]], at(*rel[k]))

    def c_in(k):
        cols = pl.ds(pl.multiple_of(128 * chip_of(*rel[k]), 128), 128)
        return remote(cf.at[k], out_ref.at[:, cols], csend.at[k], crecv.at[k], at(*rel[k]))

    order = (4, 7, 1, 2, 5, 6, 3, 0)
    for k in order:
        c_pass(k).start()

    rs_end(NCH - 1)

    def unit(first, i):
        u = first + i
        t, j, h = lax.div(u, 8), lax.div(lax.rem(u, 8), 2), lax.rem(u, 2)
        return fin[j, h, t - lax.div(9 * y - j + 3, 4)]

    for i in range(9):
        zs[i] = unit(18 * y + 9 * (1 - zh), i)
    zcopy = remote(zs, zr, zsem.at[0], zsem.at[1], far)
    zcopy.start()

    mine = (lax.broadcasted_iota(jnp.int32, (WIRE, 128), 1) < OWN) == (core == 0)
    for k in order:
        c_pass(k).wait_recv()
        full = jnp.where(mine, cs[2 * k], cp[k])
        if k == 0:
            out_ref[:, mycols] = full
        else:
            cf[k] = full
            c_copy(k).start()

    zcopy.wait_recv()
    for i in range(9):
        fg_ref[:, 128 * i : 128 * (i + 1)] = unit(18 * y + 9 * zh, i) + zr[i]

    for k in range(1, 8):
        c_in(k).wait_recv()
    zcopy.wait_send()
    for k in range(8):
        if k > 0:
            grad_copy(k).wait_send()
            c_copy(k).wait_send()
        grad_pass(k).wait_send()
        c_pass(k).wait_send()

    @pl.loop(0, NCH)
    def _(j):
        for kind in range(NK):
            x_copy(j, kind).wait_send()
        for kind in range(6):
            r_copy(j, kind).wait_send()


def on_device(images, filters, out_grad):
    img, rows, cols, chans = images.shape
    x = jnp.pad(images.reshape(ROWS, chans), ((0, WIRE - ROWS), (0, 0)))
    g = jnp.pad(out_grad.reshape(ROWS, chans), ((0, WIRE - ROWS), (0, 0)))
    vmem = pl.BlockSpec(memory_space=pltpu.VMEM)
    dma = pltpu.SemaphoreType.DMA
    out, fg = pl.pallas_call(
        kernel,
        out_shape=(jax.ShapeDtypeStruct((WIRE, chans), F32), jax.ShapeDtypeStruct((OWN, 1152), F32)),
        in_specs=[vmem] * 3,
        out_specs=(vmem, vmem),
        scratch_shapes=[
            pltpu.VMEM((NCH, NSLOT, WIRE, CW), F32),
            pltpu.VMEM((NCH, TOTAL, 3 * CW), BF16),
            pltpu.VMEM((NCH, 3 * CW, 512), BF16),
            pltpu.VMEM((NCH, 2 * CW, 128), BF16),
            pltpu.VMEM((NSLOT, WIRE, 128), F32),
            pltpu.VMEM((640, TOTAL), BF16),
            pltpu.VMEM((640, TOTAL), BF16),
            pltpu.VMEM((5, SLOT, 128), F32),
            pltpu.VMEM((5, SLOT, 128), F32),
            pltpu.VMEM((TOTAL, 640), F32),
            pltpu.VMEM((NCH, 2, 10, OWN, 128), F32),
            pltpu.VMEM((NCH, 2, 3, OWN, 128), F32),
            pltpu.VMEM((NCH, 4, 3, OWN, 128), F32),
            pltpu.VMEM((NCH, 2, 3, OWN, 128), F32),
            pltpu.VMEM((NCH, 2, 3, OWN, 128), F32),
            pltpu.VMEM((9, OWN, 128), F32),
            pltpu.VMEM((9, OWN, 128), F32),
            pltpu.VMEM((NSLOT, WIRE, 128), F32),
            pltpu.VMEM((8, WIRE, 128), F32),
            pltpu.VMEM((8, WIRE, 128), F32),
            dma((NCH, NK)), dma((NCH, NK)),
            dma((16,)), dma((16,)),
            dma((16,)), dma((16,)),
            dma((NCH, 6)), dma((NCH, 6)),
            dma((2,)),
        ],
        compiler_params=pltpu.CompilerParams(
            collective_id=0, has_side_effects=True, vmem_limit_bytes=66_000_000
        ),
    )(x, filters.reshape(OWN, 9 * chans), g)
    return out[:ROWS].reshape(img, rows, cols, chans), fg[None]


def solution(mesh):
    return jax.shard_map(
        on_device,
        mesh=mesh,
        in_specs=(
            P(("replica", "shard"), None, None, None),
            P(None, "shard", None),
            P(("replica", "shard"), None, None, None),
        ),
        out_specs=(P(("replica", "shard"), None, None, None), P(None, "shard", "replica")),
        check_vma=False,
    )
```

time: 595 us -> 118 us (0.20); the launches traced: 584 us -> 118 us
  local copies, waits for them, and re-layouts: 271 us -> 6.78 us
  matrix products: 178 us -> 0 us
  Pallas kernels: 0 us -> 110 us
  waiting for transfers between devices: 56.6 us -> 0 us
  other arithmetic: 42.9 us -> 0 us
  blocking collectives: 17.5 us -> 0 us
  between operations: 14.7 us -> 0.65 us
    dot_general x18 -> x0, matrix products: 178 us -> none  [the longest x9 110 us: tap_terms(): lax.dot_general(shifted, wslice, (((1,), (1,)), ((), ())), precision=lax....]
    reshape x11 -> x3, local copies, waits for them, and re-layouts: 123 us -> 3.34 us  [the longest x1 2 us: on_device(): return (out[:ROWS].reshape(img, rows, cols, chans), fg[None])]
    pallas_call x0 -> x1, Pallas kernels: none -> 110 us  [on_device(): pl.pallas_call(kernel, out_shape=(jax.ShapeDtypeStruct((WIRE, chans), F32...]
    slice x1 -> x0, local copies, waits for them, and re-layouts: 57.5 us -> none  [tap_terms(): shifted = padded[:, a:a + rows, c:c + cols, :].reshape(-1, width)]
    all_to_all x4 -> x0, local copies, waits for them, and re-layouts: 45.3 us -> none  [the longest x3 45.2 us: on_device(): lax.all_to_all(shaped, 'shard', split_axis=4, concat_axis=0, tiled=True)]
    psum x1 -> x0, waiting for transfers between devices: 44.2 us -> none  [on_device(): total = lax.psum(grad_sum, 'replica')]
    unnamed x8 -> x0, other arithmetic: 35 us -> none
    unnamed x50 -> x3, local copies, waits for them, and re-layouts: 32.1 us -> 1.7 us
  transfers between devices with their start and end apart: 3 -> 0, of which waited for: 2 -> 0; matrix products, arithmetic and copies ran while one was open for 34% -> 0% of each run, Pallas kernels for 0% -> 0%
where the time goes in v1:
time: 118 us
  Pallas kernels  110 us (93%)
  local copies, waits for them, and re-layouts  6.78 us (6%)
    pallas_call x1, Pallas kernels, on_device(): pl.pallas_call(kernel, out_shape=(jax.ShapeDtypeStruct((WIRE, chans), F32...  110 us

profile of v1, /device:TPU:0, one launch (start us, length us, event | category | flops | bytes accessed | tf_op | source)
XLA Modules:
  0.0 117.8 jit_solution(2217643724766511434)
XLA Ops:
  0.6 0.0 copy-start
  0.6 1.3 %reshape.16 = f32[147,1024]{1,0:T(8,128)S(1)} reshape(f32[3,7,7,1024]{3,2,1,0:T(8,128)} %param.3) | data formatting | bytes 1204224 | tf_op jit(solution)/shard_map/reshape | solution.py:391
  1.9 0.9 pad.7.x_ref
  2.8 0.0 copy-done
  2.8 0.1 reshape.18
  2.9 0.9 pad.8.g_ref
  3.7 110.3 %shard_map.50 = (f32[152,1024]{1,0:T(8,128)}, f32[64,1152]{1,0:T(8,128)}) custom-call(f32[152,1024]{1,0:T(8,128)} %pad.7.x_ref, f32[64,9216]{1,0:T(8,128)} %bitcast.3, f32[152,1024]{1,0:T(8,128)} %pad.8.g_ref), custom_call_target="tpu_custom_call" | custom-call | tf_op jit(solution)/shard_map/pallas_call | solution.py:395
  114.1 2.0 %reshape.19 = f32[3,7,7,1024]{3,2,1,0:T(8,128)} reshape(f32[147,1024]{1,0:T(8,128)} %bitcast.4) | data formatting | bytes 1204224 | tf_op jit(solution)/shard_map/reshape | solution.py:431
  116.1 1.7 %copy.6 = f32[1,64,1152]{2,1,0:T(8,128)} copy(f32[1,64,1152]{2,1,0:T(8,128)} %bitcast.5) | data formatting | bytes 589824
Async XLA Ops:
  0.6 2.1 %copy-start = (f32[3,7,7,1024]{3,2,1,0:T(8,128)S(1)}, f32[3,7,7,1024]{3,2,1,0:T(8,128)}, u32[]{:S(2)}) copy-start(f32[3,7,7,1024]{3,2,1,0:T(8,128)} %param.5) | copy-start | bytes 1806340

commit v2 on v1

--- a/solution.py
+++ b/solution.py
@@ -24,16 +24,16 @@
 OWN = 64
 DELTA = [7 * (t // 3 - 1) + (t % 3 - 1) for t in range(9)]
 
-S_OWN, S_A, S_B, S_C, S_D, S_E, S_F, S_G = 0, 2, 4, 6, 8, 10, 12, 14
+S_OWN, S_A, S_B, S_D, S_C, S_E, S_F, S_G = 0, 2, 4, 6, 8, 10, 12, 14
 K_A, K_B, K_C, K_D1, K_D2, K_E, K_F, K_G1, K_G2, K_P = range(10)
 NK = K_P + 8
 INVERSE = [0, 2, 1, 3, 4, 6, 5, 7]
 
 
 def kernel(
-    x_ref, f_ref, g_ref, out_ref, fg_ref,
-    xg, x3, f3t, f8t, gall, gsh, gsl, maskc, maskg, yacc, fgu, r1, r2, sy, fin, zs, zr, cs, cp, cf,
-    xsend, xrecv, gsend, grecv, csend, crecv, rsend, rrecv, zsem,
+    x_hbm, f_hbm, g_hbm, out_ref, fg_ref,
+    xin, gin, f_ref, x_ref, g_ref, xg, x3, f3t, f8t, gall, gsh, gsl, maskc, maskg, yacc, fgu, r1, r2, sy, fin, zs, zr, cs, cp, cf,
+    xsend, xrecv, gsend, grecv, csend, crecv, rsend, rrecv, zsend, zrecv, isem,
 ):
     rep = lax.axis_index("replica")
     shard = lax.axis_index("shard")
@@ -52,7 +52,7 @@
     def chip_of(dx, dz):
         return lax.rem(z + dz, 2) * NX + lax.rem(x + dx + NX, NX)
 
-    rel = [(0, 0), (-1, 0), (1, 0), (0, 1), (2, 0), (-1, 1), (1, 1), (2, 1)]
+    rel = [(0, 0), (-1, 0), (1, 0), (2, 0), (0, 1), (-1, 1), (1, 1), (2, 1)]
     partner = at(0, 0, 1)
     yp = lax.rem(y + 1, NY)
     ym = lax.rem(y + NY - 1, NY)
@@ -65,6 +65,18 @@
     barrier = pltpu.get_barrier_semaphore()
     for peer in peers:
         pl.semaphore_signal(barrier, inc=1, device_id=peer, device_id_type=MESH)
+
+    loads = [
+        pltpu.make_async_copy(src, dst, isem.at[i])
+        for i, (src, dst) in enumerate(((x_hbm, xin), (g_hbm, gin), (f_hbm, f_ref)))
+    ]
+    for load in loads:
+        load.start()
+    for load, src, dst in ((loads[0], xin, x_ref), (loads[1], gin, g_ref)):
+        load.wait()
+        dst[144:WIRE] = jnp.zeros((WIRE - 144, dst.shape[1]), F32)
+        for r in range(21):
+            dst[7 * r : 7 * r + 7] = src[r // 7, r % 7]
     pl.semaphore_wait(barrier, len(peers))
 
     def remote(src, dst, ssem, rsem, dev):
@@ -122,11 +134,7 @@
         for kind in (K_A, K_B, K_C, K_P):
             x_copy(j, kind).start()
 
-    for k in (4, 7, 1, 2, 5, 6, 3):
-        grad_copy(k).start()
-    grad_pass(0).start()
     x_own(0)
-    x_own(1)
 
     for j in range(NCH):
         xg[j, 0] = x_ref[:, CW * j : CW * (j + 1)]
@@ -151,6 +159,8 @@
         hi = v.astype(BF16)
         lo = (v - hi.astype(F32)).astype(BF16)
         return hi, lo
+
+    loads[2].wait()
 
     @pl.loop(0, NCH)
     def _(j):
@@ -169,12 +179,6 @@
         f8t[j, 0:CW, :] = both
         f8t[j, CW : 2 * CW, :] = both
 
-    for k in (1, 2, 3, 4, 5, 6, 7):
-        grad_in(k).wait_recv()
-        grad_pass(k).start()
-    for k in range(8):
-        grad_pass(k).wait_recv()
-
     lane4 = lax.broadcasted_iota(jnp.int32, (GROUP, 128), 1)
     low4 = lane4 < OWN
     mine4 = (lane4 < OWN) == (core == 0)
@@ -182,112 +186,172 @@
     def padded(v):
         return jnp.concatenate([v, jnp.zeros((SLOT - WIRE, v.shape[1]), v.dtype)], axis=0)
 
-    @pl.loop(0, 4)
-    def _(m):
-        g = jnp.concatenate([padded(gall[4 * m + i]) for i in range(4)], axis=0)
-        gg = jnp.where(mine4, g, pltpu.roll(g, OWN, 1))
-        cols = pl.ds(pl.multiple_of(GROUP * m, GROUP), GROUP)
-        for pair in range(5):
-            t0, t1 = 2 * pair, min(2 * pair + 1, 8)
-            first = pltpu.roll(gg, DELTA[t0] % GROUP, 0)
-            second = first if t1 == t0 else pltpu.roll(gg, DELTA[t1] % GROUP, 0)
-            mask = jnp.concatenate([maskg[pair]] * 4, axis=0)
-            hi, lo = halves((jnp.where(low4, first, second) * mask).T)
-            gsh[128 * pair : 128 * pair + 128, cols] = hi
-            gsl[128 * pair : 128 * pair + 128, cols] = lo
+    def grad_start():
+        for k in (3, 7, 1, 2, 5, 6, 4):
+            grad_copy(k).start()
+        grad_pass(0).start()
+
+    def grad_forward():
+        for k in (1, 2, 5, 6, 4, 3, 7):
+            grad_in(k).wait_recv()
+            grad_pass(k).start()
+
+    def grad_wait():
+        for k in range(8):
+            grad_pass(k).wait_recv()
+
+    def grad_stack():
+        @pl.loop(0, 4)
+        def _(m):
+            g = jnp.concatenate([padded(gall[4 * m + i]) for i in range(4)], axis=0)
+            gg = jnp.where(mine4, g, pltpu.roll(g, OWN, 1))
+            cols = pl.ds(pl.multiple_of(GROUP * m, GROUP), GROUP)
+            for pair in range(5):
+                t0, t1 = 2 * pair, min(2 * pair + 1, 8)
+                first = pltpu.roll(gg, DELTA[t0] % GROUP, 0)
+                second = first if t1 == t0 else pltpu.roll(gg, DELTA[t1] % GROUP, 0)
+                mask = jnp.concatenate([maskg[pair]] * 4, axis=0)
+                hi, lo = halves((jnp.where(low4, first, second) * mask).T)
+                gsh[128 * pair : 128 * pair + 128, cols] = hi
+                gsl[128 * pair : 128 * pair + 128, cols] = lo
 
     def window(yy, j):
-        return pl.ds(lax.div(9 * yy - j + 3, 4), 3)
-
-    def r_copy(j, kind):
-        if kind == 0:
-            src, dst, dev = fgu.at[j, 0, window(y2, j)], r1.at[j, 0], up
-        elif kind == 1:
-            src, dst, dev = fgu.at[j, 1, window(y2, j)], r1.at[j, 1], down
-        elif kind == 2:
-            src, dst, dev = fgu.at[j, 1, window(yp, j)], r2.at[j, 1], up
-        elif kind == 3:
-            src, dst, dev = fgu.at[j, 0, window(ym, j)], r2.at[j, 2], down
-        elif kind == 4:
-            src, dst, dev = sy.at[j, 0], r2.at[j, 0], up
+        return lax.div(9 * yy - j + 3, 4)
+
+    def taps3(j, h, yy):
+        return fgu[j, h, pl.ds(window(yy, j), 3)]
+
+    R_OUT = (y2, y2, yp, ym, yp, ym)
+    R_IN = (yp, ym, y, y, y, y)
+
+    def r_copy(j, kind, part):
+        span = pl.ds(2, 1) if part else pl.ds(0, 2)
+        yy = R_OUT[kind]
+        dev = down if kind in (1, 3, 5) else up
+        if kind < 4:
+            first = window(yy, j)
+            src = fgu.at[j, (0, 1, 1, 0)[kind], pl.ds(first + 2, 1) if part else pl.ds(first, 2)]
         else:
-            src, dst, dev = sy.at[j, 1], r2.at[j, 3], down
-        return remote(src, dst, rsend.at[j, kind], rrecv.at[j, kind], dev)
+            src = sy.at[j, kind - 4, span]
+        dst = r1.at[j, kind, span] if kind < 2 else r2.at[j, (None, None, 1, 2, 0, 3)[kind], span]
+        return remote(src, dst, rsend.at[j, kind, part], rrecv.at[j, kind, part], dev)
+
+    def r_start(j, kind):
+        r_copy(j, kind, 0).start()
+
+        @pl.when(R_OUT[kind] == j)
+        def _():
+            r_copy(j, kind, 1).start()
+
+    def r_recv(j, kind):
+        r_copy(j, kind, 0).wait_recv()
+
+        @pl.when(R_IN[kind] == j)
+        def _():
+            r_copy(j, kind, 1).wait_recv()
+
+    def r_sent(j, kind):
+        r_copy(j, kind, 0).wait_send()
+
+        @pl.when(R_OUT[kind] == j)
+        def _():
+            r_copy(j, kind, 1).wait_send()
 
     def rs_mid(j):
-        r_copy(j, 0).wait_recv()
-        sy[j, 0] = fgu[j, 0, window(yp, j)] + r1[j, 0]
-        r_copy(j, 4).start()
-        r_copy(j, 1).wait_recv()
-        sy[j, 1] = fgu[j, 1, window(ym, j)] + r1[j, 1]
-        r_copy(j, 5).start()
+        r_recv(j, 0)
+        sy[j, 0] = taps3(j, 0, yp) + r1[j, 0]
+        r_start(j, 4)
+        r_recv(j, 1)
+        sy[j, 1] = taps3(j, 1, ym) + r1[j, 1]
+        r_start(j, 5)
 
     def rs_end(j):
         for kind in (2, 3, 4, 5):
-            r_copy(j, kind).wait_recv()
-        fin[j, 0] = fgu[j, 0, window(y, j)] + r2[j, 0] + r2[j, 2]
-        fin[j, 1] = fgu[j, 1, window(y, j)] + r2[j, 1] + r2[j, 3]
+            r_recv(j, kind)
+        fin[j, 0] = taps3(j, 0, y) + r2[j, 0] + r2[j, 2]
+        fin[j, 1] = taps3(j, 1, y) + r2[j, 1] + r2[j, 3]
 
     def nn(a, b):
         return lax.dot_general(a, b, (((1,), (0,)), ((), ())), preferred_element_type=F32)
 
-    def conv(j, first, count):
-        @pl.loop(first, first + count)
-        def _(m):
-            rows = pl.ds(pl.multiple_of(GROUP * m, GROUP), GROUP)
-            main = nn(x3[j, rows, :], f3t[j])
-            last = nn(x3[j, rows, 0 : 2 * CW], f8t[j])
-
-            @pl.when(j == 0)
-            def _():
-                yacc[rows, 0:512] = main
-                yacc[rows, 512:640] = last
-
-            @pl.when(j > 0)
-            def _():
-                yacc[rows, 0:512] += main
-                yacc[rows, 512:640] += last
+    def unit_of(first, k):
+        i = lax.rem(k - lax.rem(first, 8) + 8, 8) if k is not None else 8
+        u = first + i
+        t, j, h = lax.div(u, 8), lax.div(lax.rem(u, 8), 2), lax.rem(u, 2)
+        return i, fin[j, h, t - lax.div(9 * y - j + 3, 4)]
+
+    first_mine = 18 * y + 9 * zh
+    first_far = 18 * y + 9 * (1 - zh)
+
+    def z_copy(j, part):
+        span = pl.ds(8, 1) if part else pl.ds(2 * j, 2)
+        return remote(zs.at[span], zr.at[span], zsend.at[j, part], zrecv.at[j, part], far)
+
+    def z_each(j, act):
+        act(z_copy(j, 0))
+
+        @pl.when(y == j)
+        def _():
+            act(z_copy(j, 1))
+
+    def z_start(j):
+        for h in range(2):
+            zs[2 * j + h] = unit_of(first_far, 2 * j + h)[1]
+
+        @pl.when(y == j)
+        def _():
+            zs[8] = unit_of(first_far, None)[1]
+
+        z_each(j, lambda copy: copy.start())
+
+    def conv_group(j, m):
+        rows = pl.ds(pl.multiple_of(GROUP * m, GROUP), GROUP)
+        main = nn(x3[j, rows, :], f3t[j])
+        last = nn(x3[j, rows, 0 : 2 * CW], f8t[j])
+
+        @pl.when(j == 0)
+        def _():
+            yacc[rows, 0:512] = main
+            yacc[rows, 512:640] = last
+
+        @pl.when(j > 0)
+        def _():
+            yacc[rows, 0:512] += main
+            yacc[rows, 512:640] += last
 
     def to_partner(j, *slots):
         for s in slots:
             x_copy(j, K_P + s // 2).start()
 
-    def chunk(j, carry):
+    def hop_one(j):
         for kind in (K_A, K_B, K_C):
             x_copy(j, kind).wait_recv()
         for kind in (K_D1, K_D2, K_E, K_F):
             x_copy(j, kind).start()
         to_partner(j, S_A, S_B, S_C)
 
-        @pl.when(j < NCH - 2)
-        def _():
-            x_own(j + 2)
-
-        @pl.when(j > 0)
-        def _():
-            conv(j - 1, 0, 2)
-
+    def hop_two(j):
         x_copy(j, K_D1).wait_recv()
         x_copy(j, K_G1).start()
         x_copy(j, K_D2).wait_recv()
         x_copy(j, K_G2).start()
+        to_partner(j, S_D)
+
+    def hop_three(j):
         x_copy(j, K_E).wait_recv()
         x_copy(j, K_F).wait_recv()
-        to_partner(j, S_D, S_E, S_F)
-
-        @pl.when(j > 0)
-        def _():
-            rs_mid(j - 1)
-            conv(j - 1, 2, 2)
-            rs_end(j - 1)
-
+        to_partner(j, S_E, S_F)
+
+    def arrive_far(j):
         x_copy(j, K_G1).wait_recv()
         x_copy(j, K_G2).wait_recv()
         to_partner(j, S_G)
-        for k in range(8):
+
+    def convert(j, half):
+        for k in range(4 * half, 4 * half + 4):
             x_copy(j, K_P + k).wait_recv()
 
-        @pl.loop(0, NSLOT)
+        @pl.loop(8 * half, 8 * half + 8)
         def _(s):
             hi, lo = halves(padded(xg[j, s]))
             rows = pl.ds(pl.multiple_of(SLOT * s, SLOT), SLOT)
@@ -295,6 +359,7 @@
             x3[j, rows, CW : 2 * CW] = lo
             x3[j, rows, 2 * CW : 3 * CW] = hi
 
+    def filter_grad(j):
         res = nn(gsh[0:576, :], x3[j, :, 0:CW])
         res += nn(gsl[0:576, :], x3[j, :, 0:CW])
         res += nn(gsh[0:576, :], x3[j, :, CW : 2 * CW])
@@ -302,18 +367,12 @@
             for t in range(9):
                 fgu[j, h, t] = res[OWN * t : OWN * (t + 1), 128 * h : 128 * (h + 1)]
             fgu[j, h, 9] = jnp.zeros((OWN, 128), F32)
-        for kind in (0, 1, 2, 3):
-            r_copy(j, kind).start()
-        return carry
-
-    lax.fori_loop(0, NCH, chunk, 0)
-
-    conv(NCH - 1, 0, 2)
-    rs_mid(NCH - 1)
-    conv(NCH - 1, 2, 2)
-
-    @pl.loop(0, 4)
-    def _(m):
+
+    def rs_start(j, kind):
+        r_start(j, kind)
+        r_start(j, kind + 1)
+
+    def tap_sum(m):
         rows = pl.ds(pl.multiple_of(GROUP * m, GROUP), GROUP)
         total = jnp.zeros((GROUP, 128), F32)
         for pair in range(5):
@@ -338,66 +397,199 @@
         cols = pl.ds(pl.multiple_of(128 * chip_of(*rel[k]), 128), 128)
         return remote(cf.at[k], out_ref.at[:, cols], csend.at[k], crecv.at[k], at(*rel[k]))
 
-    order = (4, 7, 1, 2, 5, 6, 3, 0)
-    for k in order:
-        c_pass(k).start()
-
+    def c_pass_group(m):
+        for i in range(2):
+            k = 2 * m + i
+            remote(cs.at[2 * k + 1], cp.at[k], csend.at[8 + k], crecv.at[8 + k], partner).start()
+
+    mine = (lax.broadcasted_iota(jnp.int32, (WIRE, 128), 1) < OWN) == (core == 0)
+
+    def conv_send(m):
+        for k in (2 * m, 2 * m + 1):
+            c_pass(k).wait_recv()
+            full = jnp.where(mine, cs[2 * k], cp[k])
+            if k == 0:
+                out_ref[:, mycols] = full
+            else:
+                cf[k] = full
+                c_copy(k).start()
+
+    hop_one(0)
+    x_own(1)
+    grad_start()
+    hop_two(0)
+    hop_three(0)
+    arrive_far(0)
+    convert(0, 0)
+    convert(0, 1)
+
+    @pl.loop(0, 16)
+    def _(n):
+        chunk = lax.div(n, 4)
+        group = jnp.where((n == 8) | (n == 9), n - 8, jnp.where((n == 10) | (n == 11), n - 8, 3 - lax.rem(n, 4)))
+
+        @pl.when(n == 1)
+        def _():
+            hop_one(1)
+            x_own(2)
+
+        @pl.when(n == 4)
+        def _():
+            grad_forward()
+            hop_two(1)
+            x_own(3)
+            grad_wait()
+            grad_stack()
+            hop_three(1)
+            arrive_far(1)
+
+        @pl.when(n == 6)
+        def _():
+            hop_one(3)
+
+        @pl.when(n == 7)
+        def _():
+            hop_two(2)
+
+        @pl.when(n == 8)
+        def _():
+            hop_three(2)
+            convert(2, 0)
+
+        @pl.when(n == 9)
+        def _():
+            hop_two(3)
+
+        @pl.when(n == 10)
+        def _():
+            convert(2, 1)
+
+        @pl.when(n == 12)
+        def _():
+            rs_end(1)
+            z_start(1)
+            convert(3, 0)
+            convert(3, 1)
+
+        @pl.when((n == 4) | (n == 7) | (n == 10) | (n == 12))
+        def _():
+            c = jnp.where(n == 4, 0, jnp.where(n == 7, 1, jnp.where(n == 10, 2, 3)))
+
+            @pl.when(c == 2)
+            def _():
+                rs_mid(1)
+
+            filter_grad(c)
+            rs_start(c, 0)
+
+            @pl.when((c == 1) | (c == 3))
+            def _():
+                rs_mid(c - 1)
+
+            rs_start(c, 2)
+
+            @pl.when(c == 2)
+            def _():
+                rs_end(0)
+                z_start(0)
+
+        @pl.when(n == 4)
+        def _():
+            convert(1, 0)
+            hop_one(2)
+            convert(1, 1)
+
+        @pl.when(n == 10)
+        def _():
+            hop_three(3)
+
+        conv_group(chunk, group)
+
+        @pl.when(n == 8)
+        def _():
+            arrive_far(2)
+
+        @pl.when(n == 10)
+        def _():
+            arrive_far(3)
+
+        @pl.when(n > 11)
+        def _():
+            done = 15 - n
+            tap_sum(done)
+            c_pass_group(done)
+
+            for i in range(1, 4):
+
+                @pl.when(done == 3 - i)
+                def _():
+                    conv_send(4 - i)
+                    if i == 1:
+                        rs_mid(NCH - 1)
+                    if i == 2:
+                        rs_end(NCH - 2)
+                        z_start(NCH - 2)
+
+    conv_send(0)
     rs_end(NCH - 1)
-
-    def unit(first, i):
-        u = first + i
-        t, j, h = lax.div(u, 8), lax.div(lax.rem(u, 8), 2), lax.rem(u, 2)
-        return fin[j, h, t - lax.div(9 * y - j + 3, 4)]
-
-    for i in range(9):
-        zs[i] = unit(18 * y + 9 * (1 - zh), i)
-    zcopy = remote(zs, zr, zsem.at[0], zsem.at[1], far)
-    zcopy.start()
-
-    mine = (lax.broadcasted_iota(jnp.int32, (WIRE, 128), 1) < OWN) == (core == 0)
-    for k in order:
-        c_pass(k).wait_recv()
-        full = jnp.where(mine, cs[2 * k], cp[k])
-        if k == 0:
-            out_ref[:, mycols] = full
-        else:
-            cf[k] = full
-            c_copy(k).start()
-
-    zcopy.wait_recv()
-    for i in range(9):
-        fg_ref[:, 128 * i : 128 * (i + 1)] = unit(18 * y + 9 * zh, i) + zr[i]
+    z_start(NCH - 1)
+
+    def z_wait(j):
+        z_each(j, lambda copy: copy.wait_recv())
+
+    for j in range(NCH):
+        z_wait(j)
+
+    def fg_out():
+        for k in range(8):
+            i, v = unit_of(first_mine, k)
+            fg_ref[:, pl.ds(pl.multiple_of(128 * i, 128), 128)] = v + zr[k]
+        fg_ref[:, 1024:1152] = unit_of(first_mine, None)[1] + zr[8]
+
+    fg_out()
+
+    def c_wait(k):
+        c_in(k).wait_recv()
 
     for k in range(1, 8):
-        c_in(k).wait_recv()
-    zcopy.wait_send()
-    for k in range(8):
-        if k > 0:
-            grad_copy(k).wait_send()
-            c_copy(k).wait_send()
-        grad_pass(k).wait_send()
-        c_pass(k).wait_send()
-
-    @pl.loop(0, NCH)
-    def _(j):
-        for kind in range(NK):
-            x_copy(j, kind).wait_send()
-        for kind in range(6):
-            r_copy(j, kind).wait_send()
+        c_wait(k)
+
+    def drain():
+        for k in range(8):
+            if k > 0:
+                grad_copy(k).wait_send()
+                c_copy(k).wait_send()
+            grad_pass(k).wait_send()
+            c_pass(k).wait_send()
+        for j in range(NCH):
+            z_each(j, lambda copy: copy.wait_send())
+
+        @pl.loop(0, NCH)
+        def _(j):
+            for kind in range(NK):
+                x_copy(j, kind).wait_send()
+            for kind in range(6):
+                r_sent(j, kind)
+
+    drain()
 
 
 def on_device(images, filters, out_grad):
     img, rows, cols, chans = images.shape
-    x = jnp.pad(images.reshape(ROWS, chans), ((0, WIRE - ROWS), (0, 0)))
-    g = jnp.pad(out_grad.reshape(ROWS, chans), ((0, WIRE - ROWS), (0, 0)))
+    hbm = pl.BlockSpec(memory_space=pltpu.HBM)
     vmem = pl.BlockSpec(memory_space=pltpu.VMEM)
     dma = pltpu.SemaphoreType.DMA
     out, fg = pl.pallas_call(
         kernel,
         out_shape=(jax.ShapeDtypeStruct((WIRE, chans), F32), jax.ShapeDtypeStruct((OWN, 1152), F32)),
-        in_specs=[vmem] * 3,
+        in_specs=[hbm] * 3,
         out_specs=(vmem, vmem),
         scratch_shapes=[
+            pltpu.VMEM(images.shape, F32),
+            pltpu.VMEM(out_grad.shape, F32),
+            pltpu.VMEM((OWN, 9 * chans), F32),
+            pltpu.VMEM((WIRE, chans), F32),
+            pltpu.VMEM((WIRE, chans), F32),
             pltpu.VMEM((NCH, NSLOT, WIRE, CW), F32),
             pltpu.VMEM((NCH, TOTAL, 3 * CW), BF16),
             pltpu.VMEM((NCH, 3 * CW, 512), BF16),
@@ -421,13 +613,14 @@
             dma((NCH, NK)), dma((NCH, NK)),
             dma((16,)), dma((16,)),
             dma((16,)), dma((16,)),
-            dma((NCH, 6)), dma((NCH, 6)),
-            dma((2,)),
+            dma((NCH, 6, 2)), dma((NCH, 6, 2)),
+            dma((NCH, 2)), dma((NCH, 2)),
+            dma((3,)),
         ],
         compiler_params=pltpu.CompilerParams(
             collective_id=0, has_side_effects=True, vmem_limit_bytes=66_000_000
         ),
-    )(x, filters.reshape(OWN, 9 * chans), g)
+    )(images, filters.reshape(OWN, 9 * chans), out_grad)
     return out[:ROWS].reshape(img, rows, cols, chans), fg[None]
 
 

time: 118 us -> 84.9 us (0.72)
  Pallas kernels: 110 us -> 79.5 us
  local copies, waits for them, and re-layouts: 6.78 us -> 3.69 us
    pallas_call x1, Pallas kernels: 110 us -> 79.5 us  [on_device(): pl.pallas_call(kernel, out_shape=(jax.ShapeDtypeStruct((WIRE, chans), F32...]
    pad x2 -> x0, local copies, waits for them, and re-layouts: 1.74 us -> none  [the longest x1 0.87 us: on_device(): x = jnp.pad(images.reshape(ROWS, chans), ((0, WIRE - ROWS), (0, 0)))]
    reshape x2 -> x0, local copies, waits for them, and re-layouts: 1.34 us -> none  [the longest x1 1.25 us: on_device(): x = jnp.pad(images.reshape(ROWS, chans), ((0, WIRE - ROWS), (0, 0)))]
where the time goes in v2:
time: 84.9 us; the launch traced here: 83.9 us
  Pallas kernels  79.5 us (94%)
  local copies, waits for them, and re-layouts  3.69 us (4%)
    pallas_call x1, Pallas kernels, on_device(): pl.pallas_call(kernel, out_shape=(jax.ShapeDtypeStruct((WIRE, chans), F32...  79.5 us
    reshape x1, local copies, waits for them, and re-layouts, on_device(): return (out[:ROWS].reshape(img, rows, cols, chans), fg[None])  2 us

profile of v2, /device:TPU:0, one launch (start us, length us, event | category | flops | bytes accessed | tf_op | source)
XLA Modules:
  0.0 83.9 jit_solution(8092253386849026310)
XLA Ops:
  0.6 79.5 %shard_map.50 = (f32[152,1024]{1,0:T(8,128)}, f32[64,1152]{1,0:T(8,128)}) custom-call(f32[3,7,7,1024]{3,2,1,0:T(8,128)} %x_hbm.1, f32[64,9216]{1,0:T(8,128)} %bitcast.3, f32[3,7,7,1024]{3,2,1,0:T(8,128)} %g_hbm.1), custom_call_target="tpu_custom_call" | custom-call | tf_op jit(solution)/shard_map/pallas_call | solution.py:582
  80.2 2.0 %reshape.11 = f32[3,7,7,1024]{3,2,1,0:T(8,128)} reshape(f32[147,1024]{1,0:T(8,128)} %bitcast.4) | data formatting | bytes 1204224 | tf_op jit(solution)/shard_map/reshape | solution.py:624
  82.2 1.7 %copy.6 = f32[1,64,1152]{2,1,0:T(8,128)} copy(f32[1,64,1152]{2,1,0:T(8,128)} %bitcast.5) | data formatting | bytes 589824

commit v3 on v2

--- a/solution.py
+++ b/solution.py
@@ -72,11 +72,14 @@
     ]
     for load in loads:
         load.start()
-    for load, src, dst in ((loads[0], xin, x_ref), (loads[1], gin, g_ref)):
+
+    def relayout(load, src, dst):
         load.wait()
         dst[144:WIRE] = jnp.zeros((WIRE - 144, dst.shape[1]), F32)
         for r in range(21):
             dst[7 * r : 7 * r + 7] = src[r // 7, r % 7]
+
+    relayout(loads[0], xin, x_ref)
     pl.semaphore_wait(barrier, len(peers))
 
     def remote(src, dst, ssem, rsem, dev):
@@ -135,10 +138,15 @@
             x_copy(j, kind).start()
 
     x_own(0)
+    relayout(loads[1], gin, g_ref)
 
     for j in range(NCH):
         xg[j, 0] = x_ref[:, CW * j : CW * (j + 1)]
     gall[0] = g_ref[:, pl.ds(pl.multiple_of(128 * chip_of(0, 0), 128), 128)]
+
+    @pl.loop(0, NSLOT)
+    def _(s):
+        yacc[pl.ds(pl.multiple_of(SLOT * s, SLOT), SLOT), :] = jnp.zeros((SLOT, 640), F32)
 
     lane = lax.broadcasted_iota(jnp.int32, (SLOT, 128), 1)
     low = lane < OWN
@@ -308,16 +316,8 @@
         rows = pl.ds(pl.multiple_of(GROUP * m, GROUP), GROUP)
         main = nn(x3[j, rows, :], f3t[j])
         last = nn(x3[j, rows, 0 : 2 * CW], f8t[j])
-
-        @pl.when(j == 0)
-        def _():
-            yacc[rows, 0:512] = main
-            yacc[rows, 512:640] = last
-
-        @pl.when(j > 0)
-        def _():
-            yacc[rows, 0:512] += main
-            yacc[rows, 512:640] += last
+        yacc[rows, 0:512] += main
+        yacc[rows, 512:640] += last
 
     def to_partner(j, *slots):
         for s in slots:
@@ -471,20 +471,24 @@
             convert(3, 0)
             convert(3, 1)
 
-        @pl.when((n == 4) | (n == 7) | (n == 10) | (n == 12))
+        @pl.when((n == 4) | (n == 7) | (n == 10) | (n == 13))
         def _():
             c = jnp.where(n == 4, 0, jnp.where(n == 7, 1, jnp.where(n == 10, 2, 3)))
 
-            @pl.when(c == 2)
+            @pl.when(c > 1)
             def _():
-                rs_mid(1)
+                rs_mid(c - 1)
+
+            @pl.when(c == 3)
+            def _():
+                conv_send(3)
 
             filter_grad(c)
             rs_start(c, 0)
 
-            @pl.when((c == 1) | (c == 3))
+            @pl.when(c == 1)
             def _():
-                rs_mid(c - 1)
+                rs_mid(0)
 
             rs_start(c, 2)
 
@@ -519,16 +523,16 @@
             tap_sum(done)
             c_pass_group(done)
 
-            for i in range(1, 4):
-
-                @pl.when(done == 3 - i)
-                def _():
-                    conv_send(4 - i)
-                    if i == 1:
-                        rs_mid(NCH - 1)
-                    if i == 2:
-                        rs_end(NCH - 2)
-                        z_start(NCH - 2)
+            @pl.when(n == 14)
+            def _():
+                conv_send(2)
+                rs_end(NCH - 2)
+                z_start(NCH - 2)
+
+            @pl.when(n == 15)
+            def _():
+                rs_mid(NCH - 1)
+                conv_send(1)
 
     conv_send(0)
     rs_end(NCH - 1)
@@ -572,6 +576,12 @@
                 r_sent(j, kind)
 
     drain()
+
+
+def finish(o_ref, f_ref, out_ref, fg_ref):
+    for r in range(21):
+        out_ref[r // 7, r % 7] = o_ref[7 * r : 7 * r + 7]
+    fg_ref[0] = f_ref[...]
 
 
 def on_device(images, filters, out_grad):
@@ -621,7 +631,12 @@
             collective_id=0, has_side_effects=True, vmem_limit_bytes=66_000_000
         ),
     )(images, filters.reshape(OWN, 9 * chans), out_grad)
-    return out[:ROWS].reshape(img, rows, cols, chans), fg[None]
+    return pl.pallas_call(
+        finish,
+        out_shape=(jax.ShapeDtypeStruct(images.shape, F32), jax.ShapeDtypeStruct((1, OWN, 1152), F32)),
+        in_specs=[vmem] * 2,
+        out_specs=(vmem, vmem),
+    )(out, fg)
 
 
 def solution(mesh):

time: 84.9 us -> 80.4 us (0.947); the launches traced: 83.9 us -> 80.3 us
  local copies, waits for them, and re-layouts: 3.69 us -> 0 us
    pallas_call x0 -> x1, Pallas kernels: none -> 2.21 us  [on_device(): pl.pallas_call(finish, out_shape=(jax.ShapeDtypeStruct(images.shape, F32)...]
    pallas_call x1, Pallas kernels: 79.5 us -> 77.5 us  [on_device(): pl.pallas_call(kernel, out_shape=(jax.ShapeDtypeStruct((WIRE, chans), F32...]
    reshape x1 -> x0, local copies, waits for them, and re-layouts: 2 us -> none  [on_device(): return (out[:ROWS].reshape(img, rows, cols, chans), fg[None])]
    unnamed x1 -> x0, local copies, waits for them, and re-layouts: 1.69 us -> none
where the time goes in v3:
time: 80.4 us; the launch traced here: 80.3 us
  Pallas kernels  79.7 us (99%)
    pallas_call x1, Pallas kernels, on_device(): pl.pallas_call(kernel, out_shape=(jax.ShapeDtypeStruct((WIRE, chans), F32...  77.5 us
    pallas_call x1, Pallas kernels, on_device(): pl.pallas_call(finish, out_shape=(jax.ShapeDtypeStruct(images.shape, F32)...  2.21 us

profile of v3, /device:TPU:0, one launch (start us, length us, event | category | flops | bytes accessed | tf_op | source)
XLA Modules:
  0.0 80.3 jit_solution(13278029913385997054)
XLA Ops:
  0.6 77.5 %shard_map.50 = (f32[152,1024]{1,0:T(8,128)}, f32[64,1152]{1,0:T(8,128)}) custom-call(f32[3,7,7,1024]{3,2,1,0:T(8,128)} %x_hbm.1, f32[64,9216]{1,0:T(8,128)} %bitcast.1, f32[3,7,7,1024]{3,2,1,0:T(8,128)} %g_hbm.1), custom_call_target="tpu_custom_call" | custom-call | tf_op jit(solution)/shard_map/pallas_call | solution.py:592
  78.1 2.2 %shard_map.51 = (f32[3,7,7,1024]{3,2,1,0:T(8,128)}, f32[1,64,1152]{2,1,0:T(8,128)}) custom-call(f32[152,1024]{1,0:T(8,128)} %get-tuple-element.4.o_ref, f32[64,1152]{1,0:T(8,128)} %get-tuple-element.5.f_ref), custom_call_target="tpu_custom_call" | custom-call | tf_op jit(solution)/shard_map/pallas_call | solution.py:634

commit v4 on v3

--- a/solution.py
+++ b/solution.py
@@ -509,6 +509,10 @@
 
         conv_group(chunk, group)
 
+        @pl.when(n == 15)
+        def _():
+            rs_mid(NCH - 1)
+
         @pl.when(n == 8)
         def _():
             arrive_far(2)
@@ -531,7 +535,6 @@
 
             @pl.when(n == 15)
             def _():
-                rs_mid(NCH - 1)
                 conv_send(1)
 
     conv_send(0)
@@ -578,10 +581,22 @@
     drain()
 
 
-def finish(o_ref, f_ref, out_ref, fg_ref):
-    for r in range(21):
-        out_ref[r // 7, r % 7] = o_ref[7 * r : 7 * r + 7]
-    fg_ref[0] = f_ref[...]
+def finish(o_hbm, f_hbm, out_hbm, fg_hbm, o_in, o_out, f_buf, load, store):
+    loads = [pltpu.make_async_copy(o_hbm.at[pl.ds(48 * i, 56)], o_in.at[i], load.at[i]) for i in range(3)]
+    loads.append(pltpu.make_async_copy(f_hbm, f_buf, load.at[3]))
+    stores = [pltpu.make_async_copy(o_out.at[i], out_hbm.at[i], store.at[i]) for i in range(3)]
+    stores.append(pltpu.make_async_copy(f_buf, fg_hbm.at[0], store.at[3]))
+    for copy in loads:
+        copy.start()
+    for i in range(3):
+        loads[i].wait()
+        for r in range(7):
+            o_out[i, r] = o_in[i, i + 7 * r : i + 7 * r + 7]
+        stores[i].start()
+    loads[3].wait()
+    stores[3].start()
+    for copy in stores:
+        copy.wait()
 
 
 def on_device(images, filters, out_grad):
@@ -634,8 +649,14 @@
     return pl.pallas_call(
         finish,
         out_shape=(jax.ShapeDtypeStruct(images.shape, F32), jax.ShapeDtypeStruct((1, OWN, 1152), F32)),
-        in_specs=[vmem] * 2,
-        out_specs=(vmem, vmem),
+        in_specs=[hbm] * 2,
+        out_specs=(hbm, hbm),
+        scratch_shapes=[
+            pltpu.VMEM((3, 56, chans), F32),
+            pltpu.VMEM(images.shape, F32),
+            pltpu.VMEM((OWN, 1152), F32),
+            dma((4,)), dma((4,)),
+        ],
     )(out, fg)
 
 

time: 80.4 us -> 80 us (level)
  no operation moved by 1% of the time
where the time goes in v4:
time: 80 us; the launch traced here: 79.8 us
  Pallas kernels  79.2 us (99%)
    pallas_call x1, Pallas kernels, on_device(): pl.pallas_call(kernel, out_shape=(jax.ShapeDtypeStruct((WIRE, chans), F32...  77.1 us
    pallas_call x1, Pallas kernels, on_device(): pl.pallas_call(finish, out_shape=(jax.ShapeDtypeStruct(images.shape, F32)...  2.09 us

profile of v4, /device:TPU:0, one launch (start us, length us, event | category | flops | bytes accessed | tf_op | source)
XLA Modules:
  0.0 79.8 jit_solution(959196851742743508)
XLA Ops:
  0.6 77.1 %shard_map.50 = (f32[152,1024]{1,0:T(8,128)}, f32[64,1152]{1,0:T(8,128)}) custom-call(f32[3,7,7,1024]{3,2,1,0:T(8,128)} %x_hbm.1, f32[64,9216]{1,0:T(8,128)} %bitcast.1, f32[3,7,7,1024]{3,2,1,0:T(8,128)} %g_hbm.1), custom_call_target="tpu_custom_call" | custom-call | tf_op jit(solution)/shard_map/pallas_call | solution.py:607
  77.7 2.1 %shard_map.51 = (f32[3,7,7,1024]{3,2,1,0:T(8,128)}, f32[1,64,1152]{2,1,0:T(8,128)}) custom-call(f32[152,1024]{1,0:T(8,128)} %get-tuple-element.4.o_hbm, f32[64,1152]{1,0:T(8,128)} %get-tuple-element.5.f_hbm), custom_call_target="tpu_custom_call" | custom-call | tf_op jit(solution)/shard_map/pallas_call | solution.py:649

commit v5 on v4

--- a/solution.py
+++ b/solution.py
@@ -139,6 +139,8 @@
 
     x_own(0)
     relayout(loads[1], gin, g_ref)
+    for k in (1, 2, 4):
+        grad_copy(k).start()
 
     for j in range(NCH):
         xg[j, 0] = x_ref[:, CW * j : CW * (j + 1)]
@@ -194,10 +196,9 @@
     def padded(v):
         return jnp.concatenate([v, jnp.zeros((SLOT - WIRE, v.shape[1]), v.dtype)], axis=0)
 
-    def grad_start():
-        for k in (3, 7, 1, 2, 5, 6, 4):
+    def grad_start(*chips):
+        for k in chips:
             grad_copy(k).start()
-        grad_pass(0).start()
 
     def grad_forward():
         for k in (1, 2, 5, 6, 4, 3, 7):
@@ -416,7 +417,8 @@
 
     hop_one(0)
     x_own(1)
-    grad_start()
+    grad_start(3, 7, 5, 6)
+    grad_pass(0).start()
     hop_two(0)
     hop_three(0)
     arrive_far(0)

time: 80 us -> 80.3 us (level)
  no operation moved by 1% of the time
where the time goes in v5:
time: 80.3 us; the launch traced here: 79.7 us
  Pallas kernels  79.1 us (99%)
    pallas_call x1, Pallas kernels, on_device(): pl.pallas_call(kernel, out_shape=(jax.ShapeDtypeStruct((WIRE, chans), F32...  77 us
    pallas_call x1, Pallas kernels, on_device(): pl.pallas_call(finish, out_shape=(jax.ShapeDtypeStruct(images.shape, F32)...  2.09 us

profile of v5, /device:TPU:0, one launch (start us, length us, event | category | flops | bytes accessed | tf_op | source)
XLA Modules:
  0.0 79.7 jit_solution(1055405077902311746)
XLA Ops:
  0.6 77.0 %shard_map.50 = (f32[152,1024]{1,0:T(8,128)}, f32[64,1152]{1,0:T(8,128)}) custom-call(f32[3,7,7,1024]{3,2,1,0:T(8,128)} %x_hbm.1, f32[64,9216]{1,0:T(8,128)} %bitcast.1, f32[3,7,7,1024]{3,2,1,0:T(8,128)} %g_hbm.1), custom_call_target="tpu_custom_call" | custom-call | tf_op jit(solution)/shard_map/pallas_call | solution.py:609
  77.6 2.1 %shard_map.51 = (f32[3,7,7,1024]{3,2,1,0:T(8,128)}, f32[1,64,1152]{2,1,0:T(8,128)}) custom-call(f32[152,1024]{1,0:T(8,128)} %get-tuple-element.4.o_hbm, f32[64,1152]{1,0:T(8,128)} %get-tuple-element.5.f_hbm), custom_call_target="tpu_custom_call" | custom-call | tf_op jit(solution)/shard_map/pallas_call | solution.py:651
